TPU v7x, 256 devices: a whole 4x4x8 slice. The times are simulated.
256 devices in a mesh: gx: 16 (over z, core), gy: 16 (over y, x).
Axes of the slice: x: 4, y: 4, z: 8, core: 2. Of those that a mesh axis runs over, the one named last changes fastest.
Arguments:
- populations: float32 [19, 8, 128, 2048], P(None, None, 'gy', 'gx'), may hold values from 0.49 to 22.2, as said below
- concentrations: float32 [3, 8, 128, 2048], P(None, None, 'gy', 'gx'), may hold values from 0.5 to 2
- potential: float32 [8, 128, 2048], P(None, 'gy', 'gx'), may hold values from -5 to 5
- solid_mask: int32 [8, 128, 2048], P(None, 'gy', 'gx'), may hold values 0 or 1
- surface_sign: int32 [8, 128, 2048], P(None, 'gy', 'gx'), may hold values from -1 to 1
Outputs:
- populations_new: float32 [19, 8, 128, 2048], P(None, None, 'gy', 'gx')
- concentrations_new: float32 [3, 8, 128, 2048], P(None, None, 'gy', 'gx')
- potential_new: float32 [8, 128, 2048], P(None, 'gy', 'gx')
Inputs may be any that keep to these rules, and one draw needn't show every extreme that they name: `populations`: every entry is positive, near 36 times the weight of its velocity times a density of order one. `solid_mask`: 1 marks a solid cell, 0 a fluid one. `surface_sign`: read only at solid cells.
All inputs are finite; a program needn't handle non-finite values. No bound on the sum of `solid_mask` on one device may be relied on, other than what follows from the above.
Results may differ from a plain program's by a relative error of at most 0.0018.
Values sent between devices are 32-bit elements; how exact they have to be, the bound alone decides.
No kernel may reach another device: no remote copies, remote signals or barrier semaphores. Data moves between devices by JAX's collectives and lax.ppermute only.
A program may use at most 64 MiB of HBM per device.

v0:
```python
import jax
import jax.numpy as jnp
import numpy as np
from jax import lax
from jax.sharding import PartitionSpec as P

STEPS = 4
CYCLES = 2
SSTEP = 4
lattice_velocity = (
    (0, 0, 0),
    (0, 0, 1),
    (0, 0, -1),
    (0, 1, 0),
    (0, -1, 0),
    (1, 0, 0),
    (-1, 0, 0),
    (0, 1, 1),
    (0, -1, -1),
    (0, 1, -1),
    (0, -1, 1),
    (1, 0, 1),
    (-1, 0, -1),
    (1, 0, -1),
    (-1, 0, 1),
    (1, 1, 0),
    (-1, -1, 0),
    (1, -1, 0),
    (-1, 1, 0),
)
opposite = (0, 2, 1, 4, 3, 6, 5, 8, 7, 10, 9, 12, 11, 14, 13, 16, 15, 18, 17)
lattice_weight = (1.0 / 3.0,) + (1.0 / 18.0,) * 6 + (1.0 / 36.0,) * 12
moving = (1, 2, 3, 4, 7, 8, 9, 10, 11, 12, 13, 14, 15, 16, 17, 18)
relax_time = 1.25
force_scale = 0.05
valences = (1.0, -1.0, 2.0)
diffusivity = (0.05, 0.07, 0.03)
diag_coef = 6.0001
surface_scale = 2.0


def padded_2(block, sides, width):
    for axis, dim in sides:
        count = lax.axis_size(axis)
        forward = [(i, i + 1) for i in range(count - 1)]
        forward.append((count - 1, 0))
        backward = [(target, source) for source, target in forward]
        low = lax.ppermute(
            lax.slice_in_dim(block, block.shape[dim] - width, None, axis=dim), axis, forward
        )
        high = lax.ppermute(lax.slice_in_dim(block, 0, width, axis=dim), axis, backward)
        block = jnp.concatenate([low, block, high], axis=dim)
    return block


def lattice_dot(direction, vector):
    running = None
    for axis_id in range(3):
        if direction[axis_id] != 0:
            addend = vector[axis_id] if direction[axis_id] > 0 else -vector[axis_id]
            running = addend if running is None else running + addend
    return running


def ion_charge(concentration):
    return (
        valences[0] * concentration[0]
        + valences[1] * concentration[1]
        + valences[2] * concentration[2]
    )


def collide_cells(fields, concentration, fluid_mask, efield):
    density = fields[0]
    for member in range(1, 19):
        density = density + fields[member]
    momentum = []
    for axis_id in range(3):
        running = None
        for member in range(19):
            sign_val = lattice_velocity[member][axis_id]
            if sign_val != 0:
                addend = fields[member] if sign_val > 0 else -fields[member]
                running = addend if running is None else running + addend
        momentum.append(running)
    charge = fluid_mask * ion_charge(concentration)
    forcing = [force_scale * charge * efield[axis_id] for axis_id in range(3)]
    velocity = [(momentum[axis_id] + 0.5 * forcing[axis_id]) / density for axis_id in range(3)]
    speed_sq = velocity[0] * velocity[0] + velocity[1] * velocity[1] + velocity[2] * velocity[2]
    work_rate = velocity[0] * forcing[0] + velocity[1] * forcing[1] + velocity[2] * forcing[2]
    relaxed = []
    for member in range(19):
        weight = lattice_weight[member]
        if member == 0:
            projected = jnp.zeros_like(density)
            along_force = jnp.zeros_like(density)
        else:
            projected = lattice_dot(lattice_velocity[member], velocity)
            along_force = lattice_dot(lattice_velocity[member], forcing)
        balance = (
            weight
            * density
            * (1.0 + 3.0 * projected + 4.5 * projected * projected - 1.5 * speed_sq)
        )
        source = weight * (3.0 * (along_force - work_rate) + 9.0 * projected * along_force)
        relaxed.append(
            fields[member]
            - (fields[member] - balance) / relax_time
            + (1.0 - 0.5 / relax_time) * source
        )
    return (relaxed, velocity)


def face_flux(low, high, pot_low, pot_high, vel_low, vel_high, opened):
    rates = jnp.array(diffusivity, jnp.float32).reshape(3, 1, 1, 1)
    drift = jnp.array(valences, jnp.float32).reshape(3, 1, 1, 1) * rates
    middle = 0.5 * (low + high)
    return opened * (
        -rates * (high - low)
        - drift * middle * (pot_high - pot_low)
        + 0.5 * (vel_low + vel_high) * middle
    )


def ion_step(concentration, velocity, potential, fluid_mask, ion_pad, pot_rim, fluid_rim):
    fluxes = face_flux(
        concentration,
        jnp.roll(concentration, -1, 1),
        potential,
        jnp.roll(potential, -1, 0),
        velocity[0],
        jnp.roll(velocity[0], -1, 0),
        fluid_mask * jnp.roll(fluid_mask, -1, 0),
    )
    running = fluxes - jnp.roll(fluxes, 1, 1)
    conc_in = ion_pad[:3, :, :, 1:-1]
    pot_in = pot_rim[:, :, 1:-1]
    vel_in = ion_pad[3, :, :, 1:-1]
    open_in = fluid_rim[:, :, 1:-1]
    fluxes = face_flux(
        conc_in[:, :, :-1],
        conc_in[:, :, 1:],
        pot_in[:, :-1],
        pot_in[:, 1:],
        vel_in[:, :-1],
        vel_in[:, 1:],
        open_in[:, :-1] * open_in[:, 1:],
    )
    running = running + (fluxes[:, :, 1:] - fluxes[:, :, :-1])
    conc_in = ion_pad[:3, :, 1:-1, :]
    pot_in = pot_rim[:, 1:-1, :]
    vel_in = ion_pad[4, :, 1:-1, :]
    open_in = fluid_rim[:, 1:-1, :]
    fluxes = face_flux(
        conc_in[..., :-1],
        conc_in[..., 1:],
        pot_in[..., :-1],
        pot_in[..., 1:],
        vel_in[..., :-1],
        vel_in[..., 1:],
        open_in[..., :-1] * open_in[..., 1:],
    )
    running = running + (fluxes[..., 1:] - fluxes[..., :-1])
    return concentration - running


def neighbor_sum(padded):
    core = padded[:, :, 1:-1, 1:-1]
    return (
        jnp.roll(core, -1, 1)
        + jnp.roll(core, 1, 1)
        + (padded[:, :, 2:, 1:-1] + padded[:, :, :-2, 1:-1])
        + (padded[:, :, 1:-1, 2:] + padded[:, :, 1:-1, :-2])
    )


def next_level(summed, previous):
    if previous is None:
        return -summed / 6.0
    return -summed / 3.0 - previous


def shift_table():
    order_m = 2 * SSTEP + 1
    coeffs = np.zeros((order_m, order_m), np.float32)
    for block_start in (0, SSTEP + 1):
        block_depth = SSTEP if block_start == 0 else SSTEP - 1
        for column in range(block_depth):
            coeffs[block_start + column, block_start + column] = diag_coef
            coeffs[block_start + column + 1, block_start + column] = 6.0 if column == 0 else 3.0
            if column > 0:
                coeffs[block_start + column - 1, block_start + column] = 3.0
    return coeffs


def krylov_steps(gram_matrix):
    order_m = 2 * SSTEP + 1
    highest = lax.Precision.HIGHEST
    coeffs = jnp.asarray(shift_table(), jnp.float32)
    search_co = jnp.zeros((order_m,), jnp.float32).at[0].set(1.0)
    resid_co = jnp.zeros((order_m,), jnp.float32).at[SSTEP + 1].set(1.0)
    sol_co = jnp.zeros((order_m,), jnp.float32)
    residual_sq = jnp.dot(
        resid_co, jnp.dot(gram_matrix, resid_co, precision=highest), precision=highest
    )
    for inner_id in range(SSTEP):
        image_co = jnp.dot(coeffs, search_co, precision=highest)
        step_len = residual_sq / jnp.dot(
            search_co, jnp.dot(gram_matrix, image_co, precision=highest), precision=highest
        )
        sol_co = sol_co + step_len * search_co
        resid_co = resid_co - step_len * image_co
        fresh_sq = jnp.dot(
            resid_co, jnp.dot(gram_matrix, resid_co, precision=highest), precision=highest
        )
        search_co = resid_co + fresh_sq / residual_sq * search_co
        residual_sq = fresh_sq
    return (sol_co, resid_co, search_co)


def local(populations, concentrations, potential, solid_mask, surface_sign):
    highest = lax.Precision.HIGHEST
    fluid_mask = 1.0 - solid_mask.astype(jnp.float32)
    rows_y = potential.shape[1]
    cols_x = potential.shape[2]
    rims = padded_2(jnp.stack([potential, fluid_mask]), (("gx", 3), ("gy", 2)), 1)
    pot_rim = rims[0]
    fluid_rim = rims[1]
    efield = [
        (jnp.roll(potential, 1, 0) - jnp.roll(potential, -1, 0)) * 0.5,
        (pot_rim[:, :-2, 1:-1] - pot_rim[:, 2:, 1:-1]) * 0.5,
        (pot_rim[:, 1:-1, :-2] - pot_rim[:, 1:-1, 2:]) * 0.5,
    ]
    source_open = []
    for member in range(19):
        offset = lattice_velocity[member]
        window = fluid_rim[
            :, 1 - offset[1] : 1 - offset[1] + rows_y, 1 - offset[2] : 1 - offset[2] + cols_x
        ]
        source_open.append(jnp.roll(window, offset[0], 0))
    fields = [populations[member] for member in range(19)]
    concentration = concentrations
    for time_step in range(STEPS):
        relaxed, velocity = collide_cells(fields, concentration, fluid_mask, efield)
        stacked = jnp.concatenate(
            [
                jnp.stack([relaxed[member] for member in moving]),
                concentration,
                jnp.stack([velocity[1], velocity[2]]),
            ]
        )
        lattice_pad = padded_2(stacked, (("gx", 3), ("gy", 2)), 1)
        ion_pad = lattice_pad[len(moving) :]
        arrived = []
        for member in range(19):
            offset = lattice_velocity[member]
            if member in moving:
                slot_id = moving.index(member)
                piece = lattice_pad[
                    slot_id,
                    :,
                    1 - offset[1] : 1 - offset[1] + rows_y,
                    1 - offset[2] : 1 - offset[2] + cols_x,
                ]
            else:
                piece = relaxed[member]
            arrived.append(jnp.roll(piece, offset[0], 0))
        updated = [
            jnp.where(
                fluid_mask > 0.5,
                jnp.where(source_open[member] > 0.5, arrived[member], relaxed[opposite[member]]),
                fields[member],
            )
            for member in range(19)
        ]
        concentration = ion_step(
            concentration, velocity, potential, fluid_mask, ion_pad, pot_rim, fluid_rim
        )
        fields = updated
    target = fluid_mask * ion_charge(concentration) + surface_scale * surface_sign.astype(
        jnp.float32
    ) * (1.0 - fluid_mask)
    solution = potential
    start_pad = padded_2(solution[None], (("gx", 3), ("gy", 2)), 1)
    residual = target - (diag_coef * solution - neighbor_sum(start_pad)[0])
    search = residual
    for cycle_id in range(CYCLES):
        p_levels = [search]
        r_levels = [residual]
        previous = None
        current = jnp.stack([search, residual])
        for level_id in range(SSTEP):
            if level_id == SSTEP - 1:
                current = current[:1]
            padded = padded_2(current, (("gx", 3), ("gy", 2)), 1)
            following = next_level(
                neighbor_sum(padded), None if level_id == 0 else previous[: current.shape[0]]
            )
            previous = current
            current = following
            p_levels.append(current[0])
            if current.shape[0] > 1:
                r_levels.append(current[1])
        basis = jnp.stack(p_levels + r_levels)
        local_gram = jnp.einsum("aijk,bijk->ab", basis, basis, precision=highest)
        gram_matrix = lax.psum(local_gram, ("gx", "gy"))
        sol_co, resid_co, search_co = krylov_steps(gram_matrix)
        solution = solution + jnp.tensordot(sol_co, basis, axes=1, precision=highest)
        residual = jnp.tensordot(resid_co, basis, axes=1, precision=highest)
        search = jnp.tensordot(search_co, basis, axes=1, precision=highest)
    return (jnp.stack(fields), concentration, solution)


def solution(mesh):
    placed = (
        P(None, None, "gy", "gx"),
        P(None, None, "gy", "gx"),
        P(None, "gy", "gx"),
        P(None, "gy", "gx"),
        P(None, "gy", "gx"),
    )
    return jax.shard_map(
        local,
        mesh=mesh,
        in_specs=placed,
        out_specs=(P(None, None, "gy", "gx"), P(None, None, "gy", "gx"), P(None, "gy", "gx")),
        check_vma=False,
    )
```

profile of v0, /device:TPU:1, one launch (start us, length us, event | category | flops | bytes accessed | tf_op | source)
XLA Modules:
  0.0 479.0 jit_solution(2040877553520355775)
XLA Ops:
  2.4 3.0 collective-permute-start
  11.4 3.8 collective-permute-start.3
  32.1 3.3 collective-permute-start.5
  43.5 5.4 %collective-permute-start.7 = (f32[21,8,1,130]{3,2,1,0:T(1,128)S(1)}, f32[21,8,1,130]{3,2,1,0:T(1,128)S(1)}, u32[]{:S(2)}, u32[]{:S(2)}) collective-permute-start(f32[21,8,1,130]{3,2,1,0:T(1,128)S(1)} %get-tuple-element.347), channel_id=1, source_target_pairs={{1,0},{2,1},{3,2},{4,3},{5,4},{6,5},{7,6},{8,7},{9,8},{10,9},{11,1... | collective-permute-start | bytes 262088 | tf_op jit(solution)/shard_map/ppermute | solution.py:51
  70.3 3.0 collective-permute-start.9
  79.4 5.8 %collective-permute-start.11 = (f32[21,8,1,130]{3,2,1,0:T(1,128)S(1)}, f32[21,8,1,130]{3,2,1,0:T(1,128)S(1)}, u32[]{:S(2)}, u32[]{:S(2)}) collective-permute-start(f32[21,8,1,130]{3,2,1,0:T(1,128)S(1)} %get-tuple-element.341), channel_id=1, source_target_pairs={{1,0},{2,1},{3,2},{4,3},{5,4},{6,5},{7,6},{8,7},{9,8},{10,9},{11,1... | collective-permute-start | bytes 262088 | tf_op jit(solution)/shard_map/ppermute | solution.py:51
  89.6 2.3 fusion.481
  106.0 3.1 collective-permute-start.13
  115.1 5.6 %collective-permute-start.15 = (f32[21,8,1,130]{3,2,1,0:T(1,128)S(1)}, f32[21,8,1,130]{3,2,1,0:T(1,128)S(1)}, u32[]{:S(2)}, u32[]{:S(2)}) collective-permute-start(f32[21,8,1,130]{3,2,1,0:T(1,128)S(1)} %get-tuple-element.335), channel_id=1, source_target_pairs={{1,0},{2,1},{3,2},{4,3},{5,4},{6,5},{7,6},{8,7},{9,8},{10,9},{11,1... | collective-permute-start | bytes 262088 | tf_op jit(solution)/shard_map/ppermute | solution.py:51
  121.0 2.4 collective-permute-done.14
  125.4 2.3 fusion.600
  141.5 3.2 collective-permute-start.17
  146.2 5.1 %collective-permute-start.22 = (f32[1,8,1,130]{3,2,1,0:T(1,128)}, f32[1,8,1,130]{3,2,1,0:T(1,128)}, u32[]{:S(2)}, u32[]{:S(2)}) collective-permute-start(f32[1,8,1,130]{3,2,1,0:T(1,128)} %get-tuple-element.428), channel_id=1, source_target_pairs={{1,0},{2,1},{3,2},{4,3},{5,4},{6,5},{7,6},{8,7},{9,8},{10,9},{11,1... | collective-permute-start | bytes 12488 | tf_op jit(solution)/shard_map/ppermute | solution.py:51
  156.5 4.8 %collective-permute-start.19 = (f32[21,8,1,130]{3,2,1,0:T(1,128)S(1)}, f32[21,8,1,130]{3,2,1,0:T(1,128)S(1)}, u32[]{:S(2)}, u32[]{:S(2)}) collective-permute-start(f32[21,8,1,130]{3,2,1,0:T(1,128)S(1)} %get-tuple-element.328), channel_id=1, source_target_pairs={{1,0},{2,1},{3,2},{4,3},{5,4},{6,5},{7,6},{8,7},{9,8},{10,9},{11,1... | collective-permute-start | bytes 262088 | tf_op jit(solution)/shard_map/ppermute | solution.py:51
  170.8 3.6 collective-permute-start.25
  184.3 5.2 %collective-permute-start.26 = (f32[2,8,1,130]{3,0,2,1:T(2,128)S(1)}, f32[2,8,1,130]{3,0,2,1:T(2,128)S(1)}, u32[]{:S(2)}, u32[]{:S(2)}) collective-permute-start(f32[2,8,1,130]{3,0,2,1:T(2,128)S(1)} %get-tuple-element.402), channel_id=1, source_target_pairs={{1,0},{2,1},{3,2},{4,3},{5,4},{6,5},{7,6},{8,7},{9,8},{10,9},{11,1... | collective-permute-start | bytes 24968 | tf_op jit(solution)/shard_map/ppermute | solution.py:51
  190.4 5.0 %collective-permute-done.27 = f32[2,8,1,130]{3,0,2,1:T(2,128)S(1)} collective-permute-done((f32[2,8,1,130]{3,0,2,1:T(2,128)S(1)}, f32[2,8,1,130]{3,0,2,1:T(2,128)S(1)}, u32[]{:S(2)}, u32[]{:S(2)}) %collective-permute-start.27) | collective-permute-done | bytes 8352 | tf_op jit(solution)/shard_map/ppermute | solution.py:48
  196.2 4.4 collective-permute-start.29
  204.5 3.1 collective-permute-done.31
  208.2 5.1 %collective-permute-start.33 = (f32[2,8,8,1]{3,0,2,1:T(2,128)S(1)}, f32[2,8,8,1]{3,0,2,1:T(2,128)S(1)}, u32[]{:S(2)}, u32[]{:S(2)}) collective-permute-start(f32[2,8,8,1]{3,0,2,1:T(2,128)S(1)} %get-tuple-element.487), channel_id=1, source_target_pairs={{16,0},{32,16},{48,32},{64,48},{80,64},{96,80},{112,96},{128,112},... | collective-permute-start | bytes 1544 | tf_op jit(solution)/shard_map/ppermute | solution.py:51
  217.4 3.3 collective-permute-done.35
  221.3 5.1 %collective-permute-start.37 = (f32[1,8,8,1]{3,0,2,1:T(1,128)S(1)}, f32[1,8,8,1]{3,0,2,1:T(1,128)S(1)}, u32[]{:S(2)}, u32[]{:S(2)}) collective-permute-start(f32[1,8,8,1]{3,0,2,1:T(1,128)S(1)} %get-tuple-element.481), channel_id=1, source_target_pairs={{16,0},{32,16},{48,32},{64,48},{80,64},{96,80},{112,96},{128,112},... | collective-permute-start | bytes 776 | tf_op jit(solution)/shard_map/ppermute | solution.py:51
  230.3 3.1 collective-permute-done.39
  235.1 78.9 %psum.14 = f32[9,9]{1,0:T(8,128)S(1)} all-reduce(f32[9,9]{1,0:T(8,128)S(1)} %convolution_bitcast_fusion.1), channel_id=1, replica_groups=mesh['gx'=16,'gy'=16] {'gx','gy'}, use_global_device_ids=true, to_apply=%region_0.1 | all-reduce | flops 81 | bytes 648 | tf_op jit(solution)/shard_map/psum | solution.py:306
  335.4 2.3 collective-permute-done.41
  340.5 4.5 collective-permute-done.43
  353.8 3.4 collective-permute-done.47
  358.9 3.0 collective-permute-start.49
  366.1 3.1 collective-permute-done.51
  370.8 4.2 collective-permute-start.53
  378.9 3.1 collective-permute-done.55
  383.7 77.5 %psum.15 = f32[9,9]{1,0:T(8,128)S(1)} all-reduce(f32[9,9]{1,0:T(8,128)S(1)} %convolution_bitcast_fusion), channel_id=1, replica_groups=mesh['gx'=16,'gy'=16] {'gx','gy'}, use_global_device_ids=true, to_apply=%region_1.2 | all-reduce | flops 81 | bytes 648 | tf_op jit(solution)/shard_map/psum | solution.py:306
  (940 shorter events, 182.4 us)
Async XLA Ops:
  2.4 7.5 %collective-permute-start = (f32[2,8,8,1]{3,2,1,0:T(8,128)S(1)}, f32[2,8,8,1]{3,2,1,0:T(8,128)S(1)}, u32[]{:S(2)}, u32[]{:S(2)}) collective-permute-start(f32[2,8,8,1]{3,2,1,0:T(8,128)S(1)} %get-tuple-element.495), channel_id=1, source_target_pairs={{0,16},{16,32},{32,48},{48,64},{64,80},{80,96},{96,112},{112,128},... | collective-permute-start | bytes 1544 | tf_op jit(solution)/shard_map/ppermute | solution.py:48
  6.4 138.3 %collective-permute-start.20 = (f32[1,8,8,1]{3,2,1,0:T(8,128)}, f32[1,8,8,1]{3,2,1,0:T(8,128)}, u32[]{:S(2)}, u32[]{:S(2)}) collective-permute-start(f32[1,8,8,1]{3,2,1,0:T(8,128)} %get-tuple-element.508), channel_id=1, source_target_pairs={{0,16},{16,32},{32,48},{48,64},{64,80},{80,96},{96,112},{112,128},... | collective-permute-start | bytes 776 | tf_op jit(solution)/shard_map/ppermute | solution.py:48
  7.9 136.8 %collective-permute-start.21 = (f32[1,8,8,1]{3,2,1,0:T(8,128)}, f32[1,8,8,1]{3,2,1,0:T(8,128)}, u32[]{:S(2)}, u32[]{:S(2)}) collective-permute-start(f32[1,8,8,1]{3,2,1,0:T(8,128)} %get-tuple-element.507), channel_id=1, source_target_pairs={{16,0},{32,16},{48,32},{64,48},{80,64},{96,80},{112,96},{128,112},... | collective-permute-start | bytes 776 | tf_op jit(solution)/shard_map/ppermute | solution.py:51
  10.1 6.1 %collective-permute-start.2 = (f32[2,8,1,130]{3,2,1,0:T(1,128)S(1)}, f32[2,8,1,130]{3,2,1,0:T(1,128)S(1)}, u32[]{:S(2)}, u32[]{:S(2)}) collective-permute-start(f32[2,8,1,130]{3,2,1,0:T(1,128)S(1)} %get-tuple-element.400), channel_id=1, source_target_pairs={{0,1},{1,2},{2,3},{3,4},{4,5},{5,6},{6,7},{7,8},{8,9},{9,10},{10,1... | collective-permute-start | bytes 24968 | tf_op jit(solution)/shard_map/ppermute | solution.py:48
  30.9 8.9 %collective-permute-start.4 = (f32[21,8,8,1]{0,2,3,1:T(8,128)S(1)}, f32[21,8,8,1]{0,2,3,1:T(8,128)S(1)}, u32[]{:S(2)}, u32[]{:S(2)}) collective-permute-start(f32[21,8,8,1]{0,2,3,1:T(8,128)S(1)} %copy.34), channel_id=1, source_target_pairs={{0,16},{16,32},{32,48},{48,64},{64,80},{80,96},{96,112},{112,128},... | collective-permute-start | bytes 16136 | tf_op jit(solution)/shard_map/ppermute | solution.py:48
  32.1 8.4 %collective-permute-start.5 = (f32[21,8,8,1]{0,2,3,1:T(8,128)S(1)}, f32[21,8,8,1]{0,2,3,1:T(8,128)}, u32[]{:S(2)}, u32[]{:S(2)}) collective-permute-start(f32[21,8,8,1]{0,2,3,1:T(8,128)S(1)} %copy.36), channel_id=1, source_target_pairs={{16,0},{32,16},{48,32},{64,48},{80,64},{96,80},{112,96},{128,112},... | collective-permute-start | bytes 16136 | tf_op jit(solution)/shard_map/ppermute | solution.py:51
  43.4 7.9 %collective-permute-start.6 = (f32[21,8,1,130]{3,2,1,0:T(1,128)S(1)}, f32[21,8,1,130]{3,2,1,0:T(1,128)S(1)}, u32[]{:S(2)}, u32[]{:S(2)}) collective-permute-start(f32[21,8,1,130]{3,2,1,0:T(1,128)S(1)} %get-tuple-element.346), channel_id=1, source_target_pairs={{0,1},{1,2},{2,3},{3,4},{4,5},{5,6},{6,7},{7,8},{8,9},{9,10},{10,1... | collective-permute-start | bytes 262088 | tf_op jit(solution)/shard_map/ppermute | solution.py:48
  43.5 7.8 %collective-permute-start.7 = (f32[21,8,1,130]{3,2,1,0:T(1,128)S(1)}, f32[21,8,1,130]{3,2,1,0:T(1,128)S(1)}, u32[]{:S(2)}, u32[]{:S(2)}) collective-permute-start(f32[21,8,1,130]{3,2,1,0:T(1,128)S(1)} %get-tuple-element.347), channel_id=1, source_target_pairs={{1,0},{2,1},{3,2},{4,3},{5,4},{6,5},{7,6},{8,7},{9,8},{10,9},{11,1... | collective-permute-start | bytes 262088 | tf_op jit(solution)/shard_map/ppermute | solution.py:51
  69.0 7.5 %collective-permute-start.8 = (f32[21,8,8,1]{0,2,3,1:T(8,128)S(1)}, f32[21,8,8,1]{0,2,3,1:T(8,128)S(1)}, u32[]{:S(2)}, u32[]{:S(2)}) collective-permute-start(f32[21,8,8,1]{0,2,3,1:T(8,128)S(1)} %copy.40), channel_id=1, source_target_pairs={{0,16},{16,32},{32,48},{48,64},{64,80},{80,96},{96,112},{112,128},... | collective-permute-start | bytes 16136 | tf_op jit(solution)/shard_map/ppermute | solution.py:48
  70.3 6.9 %collective-permute-start.9 = (f32[21,8,8,1]{0,2,3,1:T(8,128)S(1)}, f32[21,8,8,1]{0,2,3,1:T(8,128)S(1)}, u32[]{:S(2)}, u32[]{:S(2)}) collective-permute-start(f32[21,8,8,1]{0,2,3,1:T(8,128)S(1)} %copy.42), channel_id=1, source_target_pairs={{16,0},{32,16},{48,32},{64,48},{80,64},{96,80},{112,96},{128,112},... | collective-permute-start | bytes 16136 | tf_op jit(solution)/shard_map/ppermute | solution.py:51
  79.4 8.2 %collective-permute-start.10 = (f32[21,8,1,130]{3,2,1,0:T(1,128)S(1)}, f32[21,8,1,130]{3,2,1,0:T(1,128)S(1)}, u32[]{:S(2)}, u32[]{:S(2)}) collective-permute-start(f32[21,8,1,130]{3,2,1,0:T(1,128)S(1)} %get-tuple-element.340), channel_id=1, source_target_pairs={{0,1},{1,2},{2,3},{3,4},{4,5},{5,6},{6,7},{7,8},{8,9},{9,10},{10,1... | collective-permute-start | bytes 262088 | tf_op jit(solution)/shard_map/ppermute | solution.py:48
  79.4 8.2 %collective-permute-start.11 = (f32[21,8,1,130]{3,2,1,0:T(1,128)S(1)}, f32[21,8,1,130]{3,2,1,0:T(1,128)S(1)}, u32[]{:S(2)}, u32[]{:S(2)}) collective-permute-start(f32[21,8,1,130]{3,2,1,0:T(1,128)S(1)} %get-tuple-element.341), channel_id=1, source_target_pairs={{1,0},{2,1},{3,2},{4,3},{5,4},{6,5},{7,6},{8,7},{9,8},{10,9},{11,1... | collective-permute-start | bytes 262088 | tf_op jit(solution)/shard_map/ppermute | solution.py:51
  104.7 7.4 %collective-permute-start.12 = (f32[21,8,8,1]{0,2,3,1:T(8,128)S(1)}, f32[21,8,8,1]{0,2,3,1:T(8,128)S(1)}, u32[]{:S(2)}, u32[]{:S(2)}) collective-permute-start(f32[21,8,8,1]{0,2,3,1:T(8,128)S(1)} %copy.46), channel_id=1, source_target_pairs={{0,16},{16,32},{32,48},{48,64},{64,80},{80,96},{96,112},{112,128},... | collective-permute-start | bytes 16136 | tf_op jit(solution)/shard_map/ppermute | solution.py:48
  106.0 6.9 %collective-permute-start.13 = (f32[21,8,8,1]{0,2,3,1:T(8,128)S(1)}, f32[21,8,8,1]{0,2,3,1:T(8,128)S(1)}, u32[]{:S(2)}, u32[]{:S(2)}) collective-permute-start(f32[21,8,8,1]{0,2,3,1:T(8,128)S(1)} %copy.48), channel_id=1, source_target_pairs={{16,0},{32,16},{48,32},{64,48},{80,64},{96,80},{112,96},{128,112},... | collective-permute-start | bytes 16136 | tf_op jit(solution)/shard_map/ppermute | solution.py:51
  115.0 8.4 %collective-permute-start.14 = (f32[21,8,1,130]{3,2,1,0:T(1,128)S(1)}, f32[21,8,1,130]{3,2,1,0:T(1,128)S(1)}, u32[]{:S(2)}, u32[]{:S(2)}) collective-permute-start(f32[21,8,1,130]{3,2,1,0:T(1,128)S(1)} %get-tuple-element.334), channel_id=1, source_target_pairs={{0,1},{1,2},{2,3},{3,4},{4,5},{5,6},{6,7},{7,8},{8,9},{9,10},{10,1... | collective-permute-start | bytes 262088 | tf_op jit(solution)/shard_map/ppermute | solution.py:48
  115.1 8.3 %collective-permute-start.15 = (f32[21,8,1,130]{3,2,1,0:T(1,128)S(1)}, f32[21,8,1,130]{3,2,1,0:T(1,128)S(1)}, u32[]{:S(2)}, u32[]{:S(2)}) collective-permute-start(f32[21,8,1,130]{3,2,1,0:T(1,128)S(1)} %get-tuple-element.335), channel_id=1, source_target_pairs={{1,0},{2,1},{3,2},{4,3},{5,4},{6,5},{7,6},{8,7},{9,8},{10,9},{11,1... | collective-permute-start | bytes 262088 | tf_op jit(solution)/shard_map/ppermute | solution.py:51
  140.3 13.2 %collective-permute-start.16 = (f32[21,8,8,1]{0,2,3,1:T(8,128)S(1)}, f32[21,8,8,1]{0,2,3,1:T(8,128)S(1)}, u32[]{:S(2)}, u32[]{:S(2)}) collective-permute-start(f32[21,8,8,1]{0,2,3,1:T(8,128)S(1)} %copy.52), channel_id=1, source_target_pairs={{0,16},{16,32},{32,48},{48,64},{64,80},{80,96},{96,112},{112,128},... | collective-permute-start | bytes 16136 | tf_op jit(solution)/shard_map/ppermute | solution.py:48
  141.5 12.8 %collective-permute-start.17 = (f32[21,8,8,1]{0,2,3,1:T(8,128)S(1)}, f32[21,8,8,1]{0,2,3,1:T(8,128)S(1)}, u32[]{:S(2)}, u32[]{:S(2)}) collective-permute-start(f32[21,8,8,1]{0,2,3,1:T(8,128)S(1)} %copy.54), channel_id=1, source_target_pairs={{16,0},{32,16},{48,32},{64,48},{80,64},{96,80},{112,96},{128,112},... | collective-permute-start | bytes 16136 | tf_op jit(solution)/shard_map/ppermute | solution.py:51
  146.2 21.8 %collective-permute-start.22 = (f32[1,8,1,130]{3,2,1,0:T(1,128)}, f32[1,8,1,130]{3,2,1,0:T(1,128)}, u32[]{:S(2)}, u32[]{:S(2)}) collective-permute-start(f32[1,8,1,130]{3,2,1,0:T(1,128)} %get-tuple-element.428), channel_id=1, source_target_pairs={{1,0},{2,1},{3,2},{4,3},{5,4},{6,5},{7,6},{8,7},{9,8},{10,9},{11,1... | collective-permute-start | bytes 12488 | tf_op jit(solution)/shard_map/ppermute | solution.py:51
  151.4 16.7 %collective-permute-start.23 = (f32[1,8,1,130]{3,2,1,0:T(1,128)}, f32[1,8,1,130]{3,2,1,0:T(1,128)}, u32[]{:S(2)}, u32[]{:S(2)}) collective-permute-start(f32[1,8,1,130]{3,2,1,0:T(1,128)} %get-tuple-element.429), channel_id=1, source_target_pairs={{0,1},{1,2},{2,3},{3,4},{4,5},{5,6},{6,7},{7,8},{8,9},{9,10},{10,1... | collective-permute-start | bytes 12488 | tf_op jit(solution)/shard_map/ppermute | solution.py:48
  156.4 7.7 %collective-permute-start.18 = (f32[21,8,1,130]{3,2,1,0:T(1,128)S(1)}, f32[21,8,1,130]{3,2,1,0:T(1,128)S(1)}, u32[]{:S(2)}, u32[]{:S(2)}) collective-permute-start(f32[21,8,1,130]{3,2,1,0:T(1,128)S(1)} %get-tuple-element.329), channel_id=1, source_target_pairs={{0,1},{1,2},{2,3},{3,4},{4,5},{5,6},{6,7},{7,8},{8,9},{9,10},{10,1... | collective-permute-start | bytes 262088 | tf_op jit(solution)/shard_map/ppermute | solution.py:48
  156.5 7.6 %collective-permute-start.19 = (f32[21,8,1,130]{3,2,1,0:T(1,128)S(1)}, f32[21,8,1,130]{3,2,1,0:T(1,128)S(1)}, u32[]{:S(2)}, u32[]{:S(2)}) collective-permute-start(f32[21,8,1,130]{3,2,1,0:T(1,128)S(1)} %get-tuple-element.328), channel_id=1, source_target_pairs={{1,0},{2,1},{3,2},{4,3},{5,4},{6,5},{7,6},{8,7},{9,8},{10,9},{11,1... | collective-permute-start | bytes 262088 | tf_op jit(solution)/shard_map/ppermute | solution.py:51
  170.0 14.1 %collective-permute-start.24 = (f32[2,8,8,1]{3,0,2,1:T(2,128)S(1)}, f32[2,8,8,1]{3,0,2,1:T(2,128)S(1)}, u32[]{:S(2)}, u32[]{:S(2)}) collective-permute-start(f32[2,8,8,1]{3,0,2,1:T(2,128)S(1)} %get-tuple-element.502), channel_id=1, source_target_pairs={{0,16},{16,32},{32,48},{48,64},{64,80},{80,96},{96,112},{112,128},... | collective-permute-start | bytes 1544 | tf_op jit(solution)/shard_map/ppermute | solution.py:48
  170.8 13.4 %collective-permute-start.25 = (f32[2,8,8,1]{3,0,2,1:T(2,128)S(1)}, f32[2,8,8,1]{3,0,2,1:T(2,128)S(1)}, u32[]{:S(2)}, u32[]{:S(2)}) collective-permute-start(f32[2,8,8,1]{3,0,2,1:T(2,128)S(1)} %get-tuple-element.501), channel_id=1, source_target_pairs={{16,0},{32,16},{48,32},{64,48},{80,64},{96,80},{112,96},{128,112},... | collective-permute-start | bytes 1544 | tf_op jit(solution)/shard_map/ppermute | solution.py:51
  184.3 6.1 %collective-permute-start.26 = (f32[2,8,1,130]{3,0,2,1:T(2,128)S(1)}, f32[2,8,1,130]{3,0,2,1:T(2,128)S(1)}, u32[]{:S(2)}, u32[]{:S(2)}) collective-permute-start(f32[2,8,1,130]{3,0,2,1:T(2,128)S(1)} %get-tuple-element.402), channel_id=1, source_target_pairs={{1,0},{2,1},{3,2},{4,3},{5,4},{6,5},{7,6},{8,7},{9,8},{10,9},{11,1... | collective-permute-start | bytes 24968 | tf_op jit(solution)/shard_map/ppermute | solution.py:51
  189.5 5.9 %collective-permute-start.27 = (f32[2,8,1,130]{3,0,2,1:T(2,128)S(1)}, f32[2,8,1,130]{3,0,2,1:T(2,128)S(1)}, u32[]{:S(2)}, u32[]{:S(2)}) collective-permute-start(f32[2,8,1,130]{3,0,2,1:T(2,128)S(1)} %get-tuple-element.403), channel_id=1, source_target_pairs={{0,1},{1,2},{2,3},{3,4},{4,5},{5,6},{6,7},{7,8},{8,9},{9,10},{10,1... | collective-permute-start | bytes 24968 | tf_op jit(solution)/shard_map/ppermute | solution.py:48
  201.7 6.0 %collective-permute-start.31 = (f32[2,8,1,130]{3,0,2,1:T(2,128)S(1)}, f32[2,8,1,130]{3,0,2,1:T(2,128)S(1)}, u32[]{:S(2)}, u32[]{:S(2)}) collective-permute-start(f32[2,8,1,130]{3,0,2,1:T(2,128)S(1)} %get-tuple-element.399), channel_id=1, source_target_pairs={{0,1},{1,2},{2,3},{3,4},{4,5},{5,6},{6,7},{7,8},{8,9},{9,10},{10,1... | collective-permute-start | bytes 24968 | tf_op jit(solution)/shard_map/ppermute | solution.py:48
  208.2 6.0 %collective-permute-start.33 = (f32[2,8,8,1]{3,0,2,1:T(2,128)S(1)}, f32[2,8,8,1]{3,0,2,1:T(2,128)S(1)}, u32[]{:S(2)}, u32[]{:S(2)}) collective-permute-start(f32[2,8,8,1]{3,0,2,1:T(2,128)S(1)} %get-tuple-element.487), channel_id=1, source_target_pairs={{16,0},{32,16},{48,32},{64,48},{80,64},{96,80},{112,96},{128,112},... | collective-permute-start | bytes 1544 | tf_op jit(solution)/shard_map/ppermute | solution.py:51
  214.5 6.2 %collective-permute-start.35 = (f32[2,8,1,130]{3,0,2,1:T(2,128)S(1)}, f32[2,8,1,130]{3,0,2,1:T(2,128)S(1)}, u32[]{:S(2)}, u32[]{:S(2)}) collective-permute-start(f32[2,8,1,130]{3,0,2,1:T(2,128)S(1)} %get-tuple-element.397), channel_id=1, source_target_pairs={{0,1},{1,2},{2,3},{3,4},{4,5},{5,6},{6,7},{7,8},{8,9},{9,10},{10,1... | collective-permute-start | bytes 24968 | tf_op jit(solution)/shard_map/ppermute | solution.py:48
  221.3 6.0 %collective-permute-start.37 = (f32[1,8,8,1]{3,0,2,1:T(1,128)S(1)}, f32[1,8,8,1]{3,0,2,1:T(1,128)S(1)}, u32[]{:S(2)}, u32[]{:S(2)}) collective-permute-start(f32[1,8,8,1]{3,0,2,1:T(1,128)S(1)} %get-tuple-element.481), channel_id=1, source_target_pairs={{16,0},{32,16},{48,32},{64,48},{80,64},{96,80},{112,96},{128,112},... | collective-permute-start | bytes 776 | tf_op jit(solution)/shard_map/ppermute | solution.py:51
  351.2 6.0 %collective-permute-start.47 = (f32[2,8,1,130]{3,0,2,1:T(2,128)S(1)}, f32[2,8,1,130]{3,0,2,1:T(2,128)S(1)}, u32[]{:S(2)}, u32[]{:S(2)}) collective-permute-start(f32[2,8,1,130]{3,0,2,1:T(2,128)S(1)} %get-tuple-element.393), channel_id=1, source_target_pairs={{0,1},{1,2},{2,3},{3,4},{4,5},{5,6},{6,7},{7,8},{8,9},{9,10},{10,1... | collective-permute-start | bytes 24968 | tf_op jit(solution)/shard_map/ppermute | solution.py:48
  363.3 6.0 %collective-permute-start.51 = (f32[2,8,1,130]{3,0,2,1:T(2,128)S(1)}, f32[2,8,1,130]{3,0,2,1:T(2,128)S(1)}, u32[]{:S(2)}, u32[]{:S(2)}) collective-permute-start(f32[2,8,1,130]{3,0,2,1:T(2,128)S(1)} %get-tuple-element.391), channel_id=1, source_target_pairs={{0,1},{1,2},{2,3},{3,4},{4,5},{5,6},{6,7},{7,8},{8,9},{9,10},{10,1... | collective-permute-start | bytes 24968 | tf_op jit(solution)/shard_map/ppermute | solution.py:48
  (299 other events, 792.7 us)
where the time goes:
time: 488 us; the launch traced here: 479 us
  blocking collectives  156 us (32%)
  starting transfers between devices  104 us (21%)
  other arithmetic  70.3 us (14%)
  waiting for transfers between devices  55.8 us (11%)
  local copies, waits for them, and re-layouts  50.7 us (10%)
  between operations  25.1 us (5%)
  matrix products  17.1 us (4%)
    psum x2, blocking collectives, local(): gram_matrix = lax.psum(local_gram, ('gx', 'gy'))  156 us
    ppermute x28, starting transfers between devices, padded_2(): lax.ppermute(lax.slice_in_dim(block, 0, width, axis=dim), axis, backward)  80.6 us
    unnamed x81, other arithmetic  41.9 us
    ppermute x28, waiting for transfers between devices, padded_2(): lax.ppermute(lax.slice_in_dim(block, block.shape[dim] - width, None, axis...  41.5 us
    ppermute x28, starting transfers between devices, padded_2(): lax.ppermute(lax.slice_in_dim(block, block.shape[dim] - width, None, axis...  23 us
    unnamed x538, local copies, waits for them, and re-layouts  22.3 us
    ppermute x28, waiting for transfers between devices, padded_2(): lax.ppermute(lax.slice_in_dim(block, 0, width, axis=dim), axis, backward)  14.2 us
  transfers between devices with their start and end apart: 56, of which 35 were waited for; matrix products, arithmetic and copies ran while one was open for 18% of the time, Pallas kernels for 0%

commit v1 on v0

--- a/solution.py
+++ b/solution.py
@@ -303,7 +303,7 @@
                 r_levels.append(current[1])
         basis = jnp.stack(p_levels + r_levels)
         local_gram = jnp.einsum("aijk,bijk->ab", basis, basis, precision=highest)
-        gram_matrix = lax.psum(local_gram, ("gx", "gy"))
+        gram_matrix = lax.psum(lax.psum(local_gram, "gx"), "gy")
         sol_co, resid_co, search_co = krylov_steps(gram_matrix)
         solution = solution + jnp.tensordot(sol_co, basis, axes=1, precision=highest)
         residual = jnp.tensordot(resid_co, basis, axes=1, precision=highest)

time: 488 us -> 462 us (0.947)
  the two profiles are of different devices: /device:TPU:1 before, /device:TPU:2 now
where the time goes in v1:
time: 462 us; the launch traced here: 453 us
  blocking collectives  130 us (28%)
  starting transfers between devices  99.6 us (22%)
  other arithmetic  70.3 us (15%)
  waiting for transfers between devices  61.4 us (13%)
  local copies, waits for them, and re-layouts  50.6 us (11%)
  between operations  24.4 us (5%)
  matrix products  16.6 us (4%)
    psum x4, blocking collectives, local(): gram_matrix = lax.psum(lax.psum(local_gram, 'gx'), 'gy')  130 us
    ppermute x28, starting transfers between devices, padded_2(): lax.ppermute(lax.slice_in_dim(block, 0, width, axis=dim), axis, backward)  89.9 us
    ppermute x28, waiting for transfers between devices, padded_2(): lax.ppermute(lax.slice_in_dim(block, block.shape[dim] - width, None, axis...  43.8 us
    unnamed x81, other arithmetic  41.9 us
    unnamed x538, local copies, waits for them, and re-layouts  22.3 us
    ppermute x28, waiting for transfers between devices, padded_2(): lax.ppermute(lax.slice_in_dim(block, 0, width, axis=dim), axis, backward)  17.6 us
    ppermute x28, starting transfers between devices, padded_2(): lax.ppermute(lax.slice_in_dim(block, block.shape[dim] - width, None, axis...  9.78 us
  transfers between devices with their start and end apart: 56, of which 32 were waited for; matrix products, arithmetic and copies ran while one was open for 19% of the time, Pallas kernels for 0%

profile of v1, /device:TPU:2, one launch (start us, length us, event | category | flops | bytes accessed | tf_op | source)
XLA Modules:
  0.0 453.5 jit_solution(2147542960936348266)
XLA Ops:
  2.4 5.3 %collective-permute-start.1 = (f32[2,8,8,1]{3,2,1,0:T(8,128)S(1)}, f32[2,8,8,1]{3,2,1,0:T(8,128)S(1)}, u32[]{:S(2)}, u32[]{:S(2)}) collective-permute-start(f32[2,8,8,1]{3,2,1,0:T(8,128)S(1)} %get-tuple-element.496), channel_id=1, source_target_pairs={{16,0},{32,16},{48,32},{64,48},{80,64},{96,80},{112,96},{128,112},... | collective-permute-start | bytes 1544 | tf_op jit(solution)/shard_map/ppermute | solution.py:51
  8.4 3.0 collective-permute-start.21
  32.1 3.0 collective-permute-start.5
  46.1 2.8 collective-permute-done.6
  48.8 2.6 collective-permute-done.7
  69.6 3.0 collective-permute-start.9
  82.2 2.6 collective-permute-done.10
  104.3 3.0 collective-permute-start.13
  117.5 3.0 collective-permute-done.14
  138.3 3.0 collective-permute-start.17
  142.8 5.3 %collective-permute-start.22 = (f32[1,8,1,130]{3,2,1,0:T(1,128)}, f32[1,8,1,130]{3,2,1,0:T(1,128)}, u32[]{:S(2)}, u32[]{:S(2)}) collective-permute-start(f32[1,8,1,130]{3,2,1,0:T(1,128)} %get-tuple-element.428), channel_id=1, source_target_pairs={{1,0},{2,1},{3,2},{4,3},{5,4},{6,5},{7,6},{8,7},{9,8},{10,9},{11,1... | collective-permute-start | bytes 12488 | tf_op jit(solution)/shard_map/ppermute | solution.py:51
  153.3 5.5 %collective-permute-start.19 = (f32[21,8,1,130]{3,2,1,0:T(1,128)S(1)}, f32[21,8,1,130]{3,2,1,0:T(1,128)S(1)}, u32[]{:S(2)}, u32[]{:S(2)}) collective-permute-start(f32[21,8,1,130]{3,2,1,0:T(1,128)S(1)} %get-tuple-element.328), channel_id=1, source_target_pairs={{1,0},{2,1},{3,2},{4,3},{5,4},{6,5},{7,6},{8,7},{9,8},{10,9},{11,1... | collective-permute-start | bytes 262088 | tf_op jit(solution)/shard_map/ppermute | solution.py:51
  168.0 2.9 collective-permute-start.25
  180.9 5.4 %collective-permute-start.26 = (f32[2,8,1,130]{3,0,2,1:T(2,128)S(1)}, f32[2,8,1,130]{3,0,2,1:T(2,128)S(1)}, u32[]{:S(2)}, u32[]{:S(2)}) collective-permute-start(f32[2,8,1,130]{3,0,2,1:T(2,128)S(1)} %get-tuple-element.402), channel_id=1, source_target_pairs={{1,0},{2,1},{3,2},{4,3},{5,4},{6,5},{7,6},{8,7},{9,8},{10,9},{11,1... | collective-permute-start | bytes 24968 | tf_op jit(solution)/shard_map/ppermute | solution.py:51
  187.7 5.7 %collective-permute-done.27 = f32[2,8,1,130]{3,0,2,1:T(2,128)S(1)} collective-permute-done((f32[2,8,1,130]{3,0,2,1:T(2,128)S(1)}, f32[2,8,1,130]{3,0,2,1:T(2,128)S(1)}, u32[]{:S(2)}, u32[]{:S(2)}) %collective-permute-start.27) | collective-permute-done | bytes 8352 | tf_op jit(solution)/shard_map/ppermute | solution.py:48
  194.2 2.9 collective-permute-start.29
  199.2 5.4 %collective-permute-start.30 = (f32[2,8,1,130]{3,0,2,1:T(2,128)S(1)}, f32[2,8,1,130]{3,0,2,1:T(2,128)S(1)}, u32[]{:S(2)}, u32[]{:S(2)}) collective-permute-start(f32[2,8,1,130]{3,0,2,1:T(2,128)S(1)} %get-tuple-element.398), channel_id=1, source_target_pairs={{1,0},{2,1},{3,2},{4,3},{5,4},{6,5},{7,6},{8,7},{9,8},{10,9},{11,1... | collective-permute-start | bytes 24968 | tf_op jit(solution)/shard_map/ppermute | solution.py:51
  208.9 2.9 collective-permute-start.33
  213.9 3.5 collective-permute-start.34
  222.0 2.9 collective-permute-start.37
  226.7 3.5 collective-permute-start.38
  235.5 25.6 %psum.28 = f32[9,9]{1,0:T(8,128)S(1)} all-reduce(f32[9,9]{1,0:T(8,128)S(1)} %convolution_bitcast_fusion.1), channel_id=1, replica_groups=mesh['gx'=16,'gy'=16] {'gx'}, use_global_device_ids=true, to_apply=%region_0.1 | all-reduce | flops 81 | bytes 648 | tf_op jit(solution)/shard_map/psum | solution.py:306
  261.1 39.6 %psum.29 = f32[9,9]{1,0:T(8,128)S(1)} all-reduce(f32[9,9]{1,0:T(8,128)S(1)} %psum.28), channel_id=1, replica_groups=mesh['gx'=16,'gy'=16] {'gy'}, use_global_device_ids=true, to_apply=%region_1.2 | all-reduce | flops 81 | bytes 648 | tf_op jit(solution)/shard_map/psum | solution.py:306
  320.1 2.9 collective-permute-start.41
  329.8 2.9 collective-permute-start.45
  334.9 5.3 %collective-permute-start.46 = (f32[2,8,1,130]{3,0,2,1:T(2,128)S(1)}, f32[2,8,1,130]{3,0,2,1:T(2,128)S(1)}, u32[]{:S(2)}, u32[]{:S(2)}) collective-permute-start(f32[2,8,1,130]{3,0,2,1:T(2,128)S(1)} %get-tuple-element.392), channel_id=1, source_target_pairs={{1,0},{2,1},{3,2},{4,3},{5,4},{6,5},{7,6},{8,7},{9,8},{10,9},{11,1... | collective-permute-start | bytes 24968 | tf_op jit(solution)/shard_map/ppermute | solution.py:51
  344.5 2.9 collective-permute-start.49
  349.5 3.5 collective-permute-start.50
  357.6 2.9 collective-permute-start.53
  362.2 3.5 collective-permute-start.54
  371.0 25.6 %psum.30 = f32[9,9]{1,0:T(8,128)S(1)} all-reduce(f32[9,9]{1,0:T(8,128)S(1)} %convolution_bitcast_fusion), channel_id=1, replica_groups=mesh['gx'=16,'gy'=16] {'gx'}, use_global_device_ids=true, to_apply=%region_2.3 | all-reduce | flops 81 | bytes 648 | tf_op jit(solution)/shard_map/psum | solution.py:306
  396.6 39.7 %psum.31 = f32[9,9]{1,0:T(8,128)S(1)} all-reduce(f32[9,9]{1,0:T(8,128)S(1)} %psum.30), channel_id=1, replica_groups=mesh['gx'=16,'gy'=16] {'gy'}, use_global_device_ids=true, to_apply=%region_3.4 | all-reduce | flops 81 | bytes 648 | tf_op jit(solution)/shard_map/psum | solution.py:306
  (942 shorter events, 197.4 us)
Async XLA Ops:
  2.4 9.0 %collective-permute-start = (f32[2,8,8,1]{3,2,1,0:T(8,128)S(1)}, f32[2,8,8,1]{3,2,1,0:T(8,128)S(1)}, u32[]{:S(2)}, u32[]{:S(2)}) collective-permute-start(f32[2,8,8,1]{3,2,1,0:T(8,128)S(1)} %get-tuple-element.495), channel_id=1, source_target_pairs={{0,16},{16,32},{32,48},{48,64},{64,80},{80,96},{96,112},{112,128},... | collective-permute-start | bytes 1544 | tf_op jit(solution)/shard_map/ppermute | solution.py:48
  2.4 9.0 %collective-permute-start.1 = (f32[2,8,8,1]{3,2,1,0:T(8,128)S(1)}, f32[2,8,8,1]{3,2,1,0:T(8,128)S(1)}, u32[]{:S(2)}, u32[]{:S(2)}) collective-permute-start(f32[2,8,8,1]{3,2,1,0:T(8,128)S(1)} %get-tuple-element.496), channel_id=1, source_target_pairs={{16,0},{32,16},{48,32},{64,48},{80,64},{96,80},{112,96},{128,112},... | collective-permute-start | bytes 1544 | tf_op jit(solution)/shard_map/ppermute | solution.py:51
  8.4 132.8 %collective-permute-start.20 = (f32[1,8,8,1]{3,2,1,0:T(8,128)}, f32[1,8,8,1]{3,2,1,0:T(8,128)}, u32[]{:S(2)}, u32[]{:S(2)}) collective-permute-start(f32[1,8,8,1]{3,2,1,0:T(8,128)} %get-tuple-element.508), channel_id=1, source_target_pairs={{0,16},{16,32},{32,48},{48,64},{64,80},{80,96},{96,112},{112,128},... | collective-permute-start | bytes 776 | tf_op jit(solution)/shard_map/ppermute | solution.py:48
  8.4 132.8 %collective-permute-start.21 = (f32[1,8,8,1]{3,2,1,0:T(8,128)}, f32[1,8,8,1]{3,2,1,0:T(8,128)}, u32[]{:S(2)}, u32[]{:S(2)}) collective-permute-start(f32[1,8,8,1]{3,2,1,0:T(8,128)} %get-tuple-element.507), channel_id=1, source_target_pairs={{16,0},{32,16},{48,32},{64,48},{80,64},{96,80},{112,96},{128,112},... | collective-permute-start | bytes 776 | tf_op jit(solution)/shard_map/ppermute | solution.py:51
  31.5 7.9 %collective-permute-start.4 = (f32[21,8,8,1]{0,2,3,1:T(8,128)S(1)}, f32[21,8,8,1]{0,2,3,1:T(8,128)S(1)}, u32[]{:S(2)}, u32[]{:S(2)}) collective-permute-start(f32[21,8,8,1]{0,2,3,1:T(8,128)S(1)} %copy.34), channel_id=1, source_target_pairs={{0,16},{16,32},{32,48},{48,64},{64,80},{80,96},{96,112},{112,128},... | collective-permute-start | bytes 16136 | tf_op jit(solution)/shard_map/ppermute | solution.py:48
  32.1 8.1 %collective-permute-start.5 = (f32[21,8,8,1]{0,2,3,1:T(8,128)S(1)}, f32[21,8,8,1]{0,2,3,1:T(8,128)}, u32[]{:S(2)}, u32[]{:S(2)}) collective-permute-start(f32[21,8,8,1]{0,2,3,1:T(8,128)S(1)} %copy.36), channel_id=1, source_target_pairs={{16,0},{32,16},{48,32},{64,48},{80,64},{96,80},{112,96},{128,112},... | collective-permute-start | bytes 16136 | tf_op jit(solution)/shard_map/ppermute | solution.py:51
  43.0 5.8 %collective-permute-start.6 = (f32[21,8,1,130]{3,2,1,0:T(1,128)S(1)}, f32[21,8,1,130]{3,2,1,0:T(1,128)S(1)}, u32[]{:S(2)}, u32[]{:S(2)}) collective-permute-start(f32[21,8,1,130]{3,2,1,0:T(1,128)S(1)} %get-tuple-element.346), channel_id=1, source_target_pairs={{0,1},{1,2},{2,3},{3,4},{4,5},{5,6},{6,7},{7,8},{8,9},{9,10},{10,1... | collective-permute-start | bytes 262088 | tf_op jit(solution)/shard_map/ppermute | solution.py:48
  44.3 7.2 %collective-permute-start.7 = (f32[21,8,1,130]{3,2,1,0:T(1,128)S(1)}, f32[21,8,1,130]{3,2,1,0:T(1,128)S(1)}, u32[]{:S(2)}, u32[]{:S(2)}) collective-permute-start(f32[21,8,1,130]{3,2,1,0:T(1,128)S(1)} %get-tuple-element.347), channel_id=1, source_target_pairs={{1,0},{2,1},{3,2},{4,3},{5,4},{6,5},{7,6},{8,7},{9,8},{10,9},{11,1... | collective-permute-start | bytes 262088 | tf_op jit(solution)/shard_map/ppermute | solution.py:51
  69.1 6.6 %collective-permute-start.8 = (f32[21,8,8,1]{0,2,3,1:T(8,128)S(1)}, f32[21,8,8,1]{0,2,3,1:T(8,128)S(1)}, u32[]{:S(2)}, u32[]{:S(2)}) collective-permute-start(f32[21,8,8,1]{0,2,3,1:T(8,128)S(1)} %copy.40), channel_id=1, source_target_pairs={{0,16},{16,32},{32,48},{48,64},{64,80},{80,96},{96,112},{112,128},... | collective-permute-start | bytes 16136 | tf_op jit(solution)/shard_map/ppermute | solution.py:48
  69.6 6.8 %collective-permute-start.9 = (f32[21,8,8,1]{0,2,3,1:T(8,128)S(1)}, f32[21,8,8,1]{0,2,3,1:T(8,128)S(1)}, u32[]{:S(2)}, u32[]{:S(2)}) collective-permute-start(f32[21,8,8,1]{0,2,3,1:T(8,128)S(1)} %copy.42), channel_id=1, source_target_pairs={{16,0},{32,16},{48,32},{64,48},{80,64},{96,80},{112,96},{128,112},... | collective-permute-start | bytes 16136 | tf_op jit(solution)/shard_map/ppermute | solution.py:51
  78.5 6.2 %collective-permute-start.10 = (f32[21,8,1,130]{3,2,1,0:T(1,128)S(1)}, f32[21,8,1,130]{3,2,1,0:T(1,128)S(1)}, u32[]{:S(2)}, u32[]{:S(2)}) collective-permute-start(f32[21,8,1,130]{3,2,1,0:T(1,128)S(1)} %get-tuple-element.340), channel_id=1, source_target_pairs={{0,1},{1,2},{2,3},{3,4},{4,5},{5,6},{6,7},{7,8},{8,9},{9,10},{10,1... | collective-permute-start | bytes 262088 | tf_op jit(solution)/shard_map/ppermute | solution.py:48
  80.6 6.0 %collective-permute-start.11 = (f32[21,8,1,130]{3,2,1,0:T(1,128)S(1)}, f32[21,8,1,130]{3,2,1,0:T(1,128)S(1)}, u32[]{:S(2)}, u32[]{:S(2)}) collective-permute-start(f32[21,8,1,130]{3,2,1,0:T(1,128)S(1)} %get-tuple-element.341), channel_id=1, source_target_pairs={{1,0},{2,1},{3,2},{4,3},{5,4},{6,5},{7,6},{8,7},{9,8},{10,9},{11,1... | collective-permute-start | bytes 262088 | tf_op jit(solution)/shard_map/ppermute | solution.py:51
  103.8 6.6 %collective-permute-start.12 = (f32[21,8,8,1]{0,2,3,1:T(8,128)S(1)}, f32[21,8,8,1]{0,2,3,1:T(8,128)S(1)}, u32[]{:S(2)}, u32[]{:S(2)}) collective-permute-start(f32[21,8,8,1]{0,2,3,1:T(8,128)S(1)} %copy.46), channel_id=1, source_target_pairs={{0,16},{16,32},{32,48},{48,64},{64,80},{80,96},{96,112},{112,128},... | collective-permute-start | bytes 16136 | tf_op jit(solution)/shard_map/ppermute | solution.py:48
  104.3 6.8 %collective-permute-start.13 = (f32[21,8,8,1]{0,2,3,1:T(8,128)S(1)}, f32[21,8,8,1]{0,2,3,1:T(8,128)S(1)}, u32[]{:S(2)}, u32[]{:S(2)}) collective-permute-start(f32[21,8,8,1]{0,2,3,1:T(8,128)S(1)} %copy.48), channel_id=1, source_target_pairs={{16,0},{32,16},{48,32},{64,48},{80,64},{96,80},{112,96},{128,112},... | collective-permute-start | bytes 16136 | tf_op jit(solution)/shard_map/ppermute | solution.py:51
  113.2 7.2 %collective-permute-start.14 = (f32[21,8,1,130]{3,2,1,0:T(1,128)S(1)}, f32[21,8,1,130]{3,2,1,0:T(1,128)S(1)}, u32[]{:S(2)}, u32[]{:S(2)}) collective-permute-start(f32[21,8,1,130]{3,2,1,0:T(1,128)S(1)} %get-tuple-element.334), channel_id=1, source_target_pairs={{0,1},{1,2},{2,3},{3,4},{4,5},{5,6},{6,7},{7,8},{8,9},{9,10},{10,1... | collective-permute-start | bytes 262088 | tf_op jit(solution)/shard_map/ppermute | solution.py:48
  115.3 5.6 %collective-permute-start.15 = (f32[21,8,1,130]{3,2,1,0:T(1,128)S(1)}, f32[21,8,1,130]{3,2,1,0:T(1,128)S(1)}, u32[]{:S(2)}, u32[]{:S(2)}) collective-permute-start(f32[21,8,1,130]{3,2,1,0:T(1,128)S(1)} %get-tuple-element.335), channel_id=1, source_target_pairs={{1,0},{2,1},{3,2},{4,3},{5,4},{6,5},{7,6},{8,7},{9,8},{10,9},{11,1... | collective-permute-start | bytes 262088 | tf_op jit(solution)/shard_map/ppermute | solution.py:51
  137.7 12.6 %collective-permute-start.16 = (f32[21,8,8,1]{0,2,3,1:T(8,128)S(1)}, f32[21,8,8,1]{0,2,3,1:T(8,128)S(1)}, u32[]{:S(2)}, u32[]{:S(2)}) collective-permute-start(f32[21,8,8,1]{0,2,3,1:T(8,128)S(1)} %copy.52), channel_id=1, source_target_pairs={{0,16},{16,32},{32,48},{48,64},{64,80},{80,96},{96,112},{112,128},... | collective-permute-start | bytes 16136 | tf_op jit(solution)/shard_map/ppermute | solution.py:48
  138.3 12.8 %collective-permute-start.17 = (f32[21,8,8,1]{0,2,3,1:T(8,128)S(1)}, f32[21,8,8,1]{0,2,3,1:T(8,128)S(1)}, u32[]{:S(2)}, u32[]{:S(2)}) collective-permute-start(f32[21,8,8,1]{0,2,3,1:T(8,128)S(1)} %copy.54), channel_id=1, source_target_pairs={{16,0},{32,16},{48,32},{64,48},{80,64},{96,80},{112,96},{128,112},... | collective-permute-start | bytes 16136 | tf_op jit(solution)/shard_map/ppermute | solution.py:51
  142.8 23.2 %collective-permute-start.22 = (f32[1,8,1,130]{3,2,1,0:T(1,128)}, f32[1,8,1,130]{3,2,1,0:T(1,128)}, u32[]{:S(2)}, u32[]{:S(2)}) collective-permute-start(f32[1,8,1,130]{3,2,1,0:T(1,128)} %get-tuple-element.428), channel_id=1, source_target_pairs={{1,0},{2,1},{3,2},{4,3},{5,4},{6,5},{7,6},{8,7},{9,8},{10,9},{11,1... | collective-permute-start | bytes 12488 | tf_op jit(solution)/shard_map/ppermute | solution.py:51
  148.2 17.9 %collective-permute-start.23 = (f32[1,8,1,130]{3,2,1,0:T(1,128)}, f32[1,8,1,130]{3,2,1,0:T(1,128)}, u32[]{:S(2)}, u32[]{:S(2)}) collective-permute-start(f32[1,8,1,130]{3,2,1,0:T(1,128)} %get-tuple-element.429), channel_id=1, source_target_pairs={{0,1},{1,2},{2,3},{3,4},{4,5},{5,6},{6,7},{7,8},{8,9},{9,10},{10,1... | collective-permute-start | bytes 12488 | tf_op jit(solution)/shard_map/ppermute | solution.py:48
  153.2 8.9 %collective-permute-start.18 = (f32[21,8,1,130]{3,2,1,0:T(1,128)S(1)}, f32[21,8,1,130]{3,2,1,0:T(1,128)S(1)}, u32[]{:S(2)}, u32[]{:S(2)}) collective-permute-start(f32[21,8,1,130]{3,2,1,0:T(1,128)S(1)} %get-tuple-element.329), channel_id=1, source_target_pairs={{0,1},{1,2},{2,3},{3,4},{4,5},{5,6},{6,7},{7,8},{8,9},{9,10},{10,1... | collective-permute-start | bytes 262088 | tf_op jit(solution)/shard_map/ppermute | solution.py:48
  153.3 8.8 %collective-permute-start.19 = (f32[21,8,1,130]{3,2,1,0:T(1,128)S(1)}, f32[21,8,1,130]{3,2,1,0:T(1,128)S(1)}, u32[]{:S(2)}, u32[]{:S(2)}) collective-permute-start(f32[21,8,1,130]{3,2,1,0:T(1,128)S(1)} %get-tuple-element.328), channel_id=1, source_target_pairs={{1,0},{2,1},{3,2},{4,3},{5,4},{6,5},{7,6},{8,7},{9,8},{10,9},{11,1... | collective-permute-start | bytes 262088 | tf_op jit(solution)/shard_map/ppermute | solution.py:51
  168.0 12.7 %collective-permute-start.24 = (f32[2,8,8,1]{3,0,2,1:T(2,128)S(1)}, f32[2,8,8,1]{3,0,2,1:T(2,128)S(1)}, u32[]{:S(2)}, u32[]{:S(2)}) collective-permute-start(f32[2,8,8,1]{3,0,2,1:T(2,128)S(1)} %get-tuple-element.502), channel_id=1, source_target_pairs={{0,16},{16,32},{32,48},{48,64},{64,80},{80,96},{96,112},{112,128},... | collective-permute-start | bytes 1544 | tf_op jit(solution)/shard_map/ppermute | solution.py:48
  168.0 12.7 %collective-permute-start.25 = (f32[2,8,8,1]{3,0,2,1:T(2,128)S(1)}, f32[2,8,8,1]{3,0,2,1:T(2,128)S(1)}, u32[]{:S(2)}, u32[]{:S(2)}) collective-permute-start(f32[2,8,8,1]{3,0,2,1:T(2,128)S(1)} %get-tuple-element.501), channel_id=1, source_target_pairs={{16,0},{32,16},{48,32},{64,48},{80,64},{96,80},{112,96},{128,112},... | collective-permute-start | bytes 1544 | tf_op jit(solution)/shard_map/ppermute | solution.py:51
  180.9 6.9 %collective-permute-start.26 = (f32[2,8,1,130]{3,0,2,1:T(2,128)S(1)}, f32[2,8,1,130]{3,0,2,1:T(2,128)S(1)}, u32[]{:S(2)}, u32[]{:S(2)}) collective-permute-start(f32[2,8,1,130]{3,0,2,1:T(2,128)S(1)} %get-tuple-element.402), channel_id=1, source_target_pairs={{1,0},{2,1},{3,2},{4,3},{5,4},{6,5},{7,6},{8,7},{9,8},{10,9},{11,1... | collective-permute-start | bytes 24968 | tf_op jit(solution)/shard_map/ppermute | solution.py:51
  186.3 7.1 %collective-permute-start.27 = (f32[2,8,1,130]{3,0,2,1:T(2,128)S(1)}, f32[2,8,1,130]{3,0,2,1:T(2,128)S(1)}, u32[]{:S(2)}, u32[]{:S(2)}) collective-permute-start(f32[2,8,1,130]{3,0,2,1:T(2,128)S(1)} %get-tuple-element.403), channel_id=1, source_target_pairs={{0,1},{1,2},{2,3},{3,4},{4,5},{5,6},{6,7},{7,8},{8,9},{9,10},{10,1... | collective-permute-start | bytes 24968 | tf_op jit(solution)/shard_map/ppermute | solution.py:48
  199.2 6.9 %collective-permute-start.30 = (f32[2,8,1,130]{3,0,2,1:T(2,128)S(1)}, f32[2,8,1,130]{3,0,2,1:T(2,128)S(1)}, u32[]{:S(2)}, u32[]{:S(2)}) collective-permute-start(f32[2,8,1,130]{3,0,2,1:T(2,128)S(1)} %get-tuple-element.398), channel_id=1, source_target_pairs={{1,0},{2,1},{3,2},{4,3},{5,4},{6,5},{7,6},{8,7},{9,8},{10,9},{11,1... | collective-permute-start | bytes 24968 | tf_op jit(solution)/shard_map/ppermute | solution.py:51
  208.9 4.9 %collective-permute-start.32 = (f32[2,8,8,1]{3,0,2,1:T(2,128)S(1)}, f32[2,8,8,1]{3,0,2,1:T(2,128)S(1)}, u32[]{:S(2)}, u32[]{:S(2)}) collective-permute-start(f32[2,8,8,1]{3,0,2,1:T(2,128)S(1)} %get-tuple-element.488), channel_id=1, source_target_pairs={{0,16},{16,32},{32,48},{48,64},{64,80},{80,96},{96,112},{112,128},... | collective-permute-start | bytes 1544 | tf_op jit(solution)/shard_map/ppermute | solution.py:48
  213.9 4.9 %collective-permute-start.34 = (f32[2,8,1,130]{3,0,2,1:T(2,128)S(1)}, f32[2,8,1,130]{3,0,2,1:T(2,128)S(1)}, u32[]{:S(2)}, u32[]{:S(2)}) collective-permute-start(f32[2,8,1,130]{3,0,2,1:T(2,128)S(1)} %get-tuple-element.396), channel_id=1, source_target_pairs={{1,0},{2,1},{3,2},{4,3},{5,4},{6,5},{7,6},{8,7},{9,8},{10,9},{11,1... | collective-permute-start | bytes 24968 | tf_op jit(solution)/shard_map/ppermute | solution.py:51
  320.0 4.9 %collective-permute-start.40 = (f32[2,8,8,1]{3,0,2,1:T(2,128)S(1)}, f32[2,8,8,1]{3,0,2,1:T(2,128)S(1)}, u32[]{:S(2)}, u32[]{:S(2)}) collective-permute-start(f32[2,8,8,1]{3,0,2,1:T(2,128)S(1)} %get-tuple-element.469), channel_id=1, source_target_pairs={{0,16},{16,32},{32,48},{48,64},{64,80},{80,96},{96,112},{112,128},... | collective-permute-start | bytes 1544 | tf_op jit(solution)/shard_map/ppermute | solution.py:48
  334.9 6.7 %collective-permute-start.46 = (f32[2,8,1,130]{3,0,2,1:T(2,128)S(1)}, f32[2,8,1,130]{3,0,2,1:T(2,128)S(1)}, u32[]{:S(2)}, u32[]{:S(2)}) collective-permute-start(f32[2,8,1,130]{3,0,2,1:T(2,128)S(1)} %get-tuple-element.392), channel_id=1, source_target_pairs={{1,0},{2,1},{3,2},{4,3},{5,4},{6,5},{7,6},{8,7},{9,8},{10,9},{11,1... | collective-permute-start | bytes 24968 | tf_op jit(solution)/shard_map/ppermute | solution.py:51
  349.5 4.9 %collective-permute-start.50 = (f32[2,8,1,130]{3,0,2,1:T(2,128)S(1)}, f32[2,8,1,130]{3,0,2,1:T(2,128)S(1)}, u32[]{:S(2)}, u32[]{:S(2)}) collective-permute-start(f32[2,8,1,130]{3,0,2,1:T(2,128)S(1)} %get-tuple-element.390), channel_id=1, source_target_pairs={{1,0},{2,1},{3,2},{4,3},{5,4},{6,5},{7,6},{8,7},{9,8},{10,9},{11,1... | collective-permute-start | bytes 24968 | tf_op jit(solution)/shard_map/ppermute | solution.py:51
  (299 other events, 717.0 us)
